TPU v7x, 512 devices: a whole 4x4x16 slice. The times are simulated.
512 devices in a mesh: dp: 8 (over z_hi, x), seq: 64 (over z_lo, y, core).
Axes of the slice: x: 4, y: 4, z: 16 (z_hi: 2, z_lo: 8; z = z_hi * 8 + z_lo), core: 2. Of those that a mesh axis runs over, the one named last changes fastest.
Arguments:
- queries: bfloat16 [32768, 2048], P('seq', 'dp'), may hold values from -15 to 15
- key_rows: bfloat16 [32768, 2048], P('seq', 'dp'), may hold values from -15 to 15
- value_rows: bfloat16 [32768, 2048], P('seq', 'dp'), may hold values from -6 to 6
- slot_queries: bfloat16 [256, 2048], P(None, 'dp'), may hold values from -15 to 15
- gate_logit: float32 [64, 2048], P('seq', 'dp'), may hold values from -6.5 to 6.5
- out_weight: bfloat16 [2048, 2048], P(None, 'dp'), may hold values from -0.1875 to 0.1875
Outputs:
- mixed: bfloat16 [2048, 32768], P('dp', 'seq')
All inputs are finite; a program needn't handle non-finite values.
Results may differ from a plain program's by a relative error of at most 0.017.
Values may be sent and summed in bfloat16 or wider, within the bound.
A program may use at most 64 MiB of HBM per device.

v0:
```python
import jax
import jax.numpy as jnp
from jax import lax
from jax.sharding import PartitionSpec as P

HEAD = 128


def from_behind(block, axis, distance):
    devices = range(lax.axis_size(axis))
    route = [(i - distance, i) for i in devices if i - distance in devices]
    return lax.ppermute(block, axis, route)


def entering(array, axis, combine, identity):
    peers, place = (lax.axis_size(axis), lax.axis_index(axis))
    everything = jax.tree.map(
        lambda part, kind: lax.all_gather(part.astype(kind), axis),
        array,
        (jnp.bfloat16, jnp.bfloat16),
    )
    start = jax.tree.map(
        lambda part, zero: jnp.broadcast_to(jnp.asarray(zero, part.dtype), part.shape),
        array,
        identity,
    )

    def turn(k, before):
        reached = k < place
        new = combine(
            before, jax.tree.map(lambda part, own: part[k].astype(own.dtype), everything, array)
        )
        return jax.tree.map(lambda a, b: jnp.where(reached, a, b), new, before)

    return lax.fori_loop(0, peers, turn, start)


def attend(query_part, key_part, value_part, allowed):
    row_count = query_part.shape[0]
    key_count = key_part.shape[0]
    head_count = query_part.shape[1] // HEAD
    queries = query_part.reshape(row_count, head_count, HEAD)
    keyset = key_part.reshape(key_count, head_count, HEAD)
    valset = value_part.reshape(key_count, head_count, HEAD)
    scores = jnp.einsum(
        "rhe,she->hrs", queries, keyset, preferred_element_type=jnp.float32
    ) * HEAD ** (-0.5)
    if allowed is not None:
        scores = jnp.where(allowed[None], scores, -1e30)
    highest = jnp.max(scores, axis=-1, keepdims=True)
    weights = jnp.exp(scores - highest)
    totals = jnp.sum(weights, axis=-1, keepdims=True)
    summed = jnp.einsum(
        "hrs,she->rhe", weights.astype(jnp.bfloat16), valset, preferred_element_type=jnp.float32
    )
    return (summed / jnp.transpose(totals, (1, 0, 2))).reshape(row_count, head_count * HEAD)


def compose(earlier_map, later_map):
    return (earlier_map[0] * later_map[0], later_map[0] * earlier_map[1] + later_map[1])


def body(queries, key_rows, value_rows, slot_queries, gate_logit, out_weight):
    keep_rate = jax.nn.sigmoid(gate_logit[0])
    stacked = jnp.stack([key_rows, value_rows], axis=0)
    previous = from_behind(stacked, "seq", 1)
    updates = attend(slot_queries, key_rows, value_rows, None)
    identity = (jnp.ones_like(keep_rate), jnp.zeros_like(updates))
    prefix = entering((keep_rate, (1.0 - keep_rate) * updates), "seq", compose, identity)
    carried = prefix[1]
    memory = carried.astype(jnp.bfloat16)
    key_all = jnp.concatenate([memory, previous[0], key_rows], axis=0)
    value_all = jnp.concatenate([memory, previous[1], value_rows], axis=0)
    tokens = queries.shape[0]
    row_index = lax.broadcasted_iota(jnp.int32, (tokens, tokens), 0)
    col_index = lax.broadcasted_iota(jnp.int32, (tokens, tokens), 1)
    later_block = lax.axis_index("seq") > 0
    state_cols = jnp.ones((tokens, memory.shape[0]), jnp.bool_)
    allowed = jnp.concatenate(
        [state_cols, (col_index > row_index) & later_block, col_index <= row_index], axis=1
    )
    attended = attend(queries, key_all, value_all, allowed).astype(jnp.bfloat16)
    return lax.psum_scatter(
        lax.dot_general(
            out_weight, attended, (((1,), (1,)), ((), ())), preferred_element_type=jnp.float32
        ).astype(jnp.bfloat16),
        "dp",
        scatter_dimension=0,
        tiled=True,
    )


def solution(mesh):
    in_specs = (
        P("seq", "dp"),
        P("seq", "dp"),
        P("seq", "dp"),
        P(None, "dp"),
        P("seq", "dp"),
        P(None, "dp"),
    )
    out_specs = P("dp", "seq")
    return jax.shard_map(body, mesh=mesh, in_specs=in_specs, out_specs=out_specs, check_vma=False)
```

profile of v0, /device:TPU:8, one launch (start us, length us, event | category | flops | bytes accessed | tf_op | source)
XLA Modules:
  0.0 412.1 jit_solution(9282224714616615)
XLA Ops:
  6.5 1.2 copy.43
  7.7 1.1 copy.46
  8.8 1.3 fusion.39
  12.7 1.9 collective-permute-start
  15.6 117.4 %all-gather = bf16[64,1,256]{2,1,0:T(2,128)(2,1)S(1)} all-gather(bf16[1,1,256]{2,1,0:T(2,128)(2,1)S(1)} %bitcast.85), channel_id=1, replica_groups=mesh['dp'=8,'seq'=64] {'seq'}, dimensions={0}, use_global_device_ids=true | all-gather | bytes 33280 | tf_op jit(solution)/shard_map/all_gather | solution.py:18
  134.3 7.7 %all-gather.3.cloned.1.call-done = bf16[64,256,256]{2,1,0:T(8,128)(2,1)} async-done(((bf16[1,256,256]{2,1,0:T(8,128)(2,1)}), bf16[64,256,256]{2,1,0:T(8,128)(2,1)}) %all-gather.3.cloned.1.call-update) | async-done | bytes 8388624 | tf_op jit(solution)/shard_map/all_gather | solution.py:18
  142.0 111.5 %while.14 = (s32[]{:T(128)}, f32[256,256]{1,0:T(8,128)S(1)}, s32[]{:T(128)}, bf16[64,256]{1,0:T(8,128)(2,1)}, bf16[64,256,256]{2,1,0:T(8,128)(2,1)}, /*index=5*/s32[]{:T(128)}, s32[]{:T(128)}) while((s32[]{:T(128)}, f32[256,256]{1,0:T(8,128)S(1)}, s32[]{:T(128)}, bf16[64,256]{1,0:T(8,128)(2,1)}, bf16[64,256,256]{2,1,0:T(8,128)(2,1)}, ...), condition=%wide.region_3.4_spmd.clone, body=%wide.region_2.3_spmd.clone.sunk | while | flops 327940 | bytes 658025 | solution.py:35
  142.7 1.0 fusion.48
  144.4 1.0 fusion.48
  146.2 1.0 fusion.48
  147.9 1.0 fusion.48
  149.7 1.0 fusion.48
  151.4 1.0 fusion.48
  153.1 1.0 fusion.48
  154.9 1.0 fusion.48
  156.6 1.0 fusion.48
  158.4 1.0 fusion.48
  160.1 1.0 fusion.48
  161.9 1.0 fusion.48
  163.6 1.0 fusion.48
  165.4 1.0 fusion.48
  167.1 1.0 fusion.48
  168.9 1.0 fusion.48
  170.6 1.0 fusion.48
  172.3 1.0 fusion.48
  174.1 1.0 fusion.48
  175.8 1.0 fusion.48
  177.6 1.0 fusion.48
  179.3 1.0 fusion.48
  181.0 1.0 fusion.48
  182.8 1.0 fusion.48
  184.5 1.0 fusion.48
  186.2 1.0 fusion.48
  188.0 1.0 fusion.48
  189.7 1.0 fusion.48
  191.5 1.0 fusion.48
  193.2 1.0 fusion.48
  194.9 1.0 fusion.48
  198.4 1.0 fusion.48
  200.2 1.0 fusion.48
  203.6 1.0 fusion.48
  205.4 1.0 fusion.48
  208.9 1.0 fusion.48
  210.6 1.0 fusion.48
  212.3 1.0 fusion.48
  215.8 1.0 fusion.48
  217.6 1.0 fusion.48
  221.0 1.0 fusion.48
  222.8 1.0 fusion.48
  226.3 1.0 fusion.48
  228.0 1.0 fusion.48
  229.8 1.0 fusion.48
  231.5 1.0 fusion.48
  233.3 1.0 fusion.48
  235.0 1.0 fusion.48
  238.5 1.0 fusion.48
  240.2 1.0 fusion.48
  242.0 1.0 fusion.48
  243.7 1.0 fusion.48
  253.8 2.1 fusion.40
  256.6 1.0 fusion.14
  257.7 2.1 fusion.3
  259.8 143.7 %reduce-scatter.2.cloned.1.call-done = bf16[256,512]{0,1:T(8,128)(2,1)} async-done(((bf16[2048,512]{0,1:T(8,128)(2,1)}), bf16[256,512]{0,1:T(8,128)(2,1)}) %reduce-scatter.2.cloned.1.call-update) | async-done | bytes 262160 | tf_op jit(solution)/shard_map/reduce_scatter | solution.py:83
  403.5 1.8 copy.56
  (105 shorter events, 62.1 us)
Async XLA Ops:
  6.5 251.1 %copy-start = (bf16[2048,256]{1,0:T(8,128)(2,1)S(1)}, bf16[2048,256]{1,0:T(8,128)(2,1)}, u32[]{:S(2)}) copy-start(bf16[2048,256]{1,0:T(8,128)(2,1)} %param.13) | copy-start | bytes 3145732
  6.5 4.5 %copy-start.2 = (f32[1,256]{1,0:T(1,128)S(1)}, f32[1,256]{1,0:T(1,128)}, u32[]{:S(2)}) copy-start(f32[1,256]{1,0:T(1,128)} %param.12) | copy-start | bytes 3076
  6.5 135.5 %all-gather.3.cloned.1.call-start = ((), (), s32[]{:S(2)}) async-start(), calls=%async_computation.1 | async-start | bytes 8519680 | tf_op jit(solution)/shard_map/all_gather | solution.py:18
  11.7 391.8 %reduce-scatter.2.cloned.1.call-start = ((), (), s32[]{:S(2)}) async-start(), calls=%async_computation.2 | async-start | bytes 2359296 | tf_op jit(solution)/shard_map/reduce_scatter | solution.py:83
  12.7 121.4 %collective-permute-start = (bf16[2,512,256]{1,2,0:T(8,128)(2,1)}, bf16[2,512,256]{1,2,0:T(8,128)(2,1)S(1)}, u32[]{:S(2)}, u32[]{:S(2)}) collective-permute-start(bf16[2,512,256]{1,2,0:T(8,128)(2,1)} %pad_maximum_fusion), channel_id=1, source_target_pairs={{0,1},{1,2},{2,3},{3,4},{4,5},{5,6},{6,7},{7,8},{8,9},{9,10},{10,1... | collective-permute-start | bytes 1572872 | tf_op jit(solution)/shard_map/ppermute | solution.py:12
  134.1 119.7 %copy-start.1 = (bf16[512,2,128]{2,0,1:T(8,128)(2,1)S(1)}, bf16[512,2,128]{2,0,1:T(8,128)(2,1)}, u32[]{:S(2)}) copy-start(bf16[512,2,128]{2,0,1:T(8,128)(2,1)} %copy.53) | copy-start | bytes 786436
Sparse Core Ops, SparseCore 0:
  11.9 130.1 all-gather.2
  259.9 143.5 reduce-scatter.1
where the time goes:
time: 416 us; the launch traced here: 412 us
  waiting for transfers between devices  151 us (36%)
  blocking collectives  117 us (28%)
  other arithmetic  114 us (27%)
  between operations  13.6 us (3%)
  matrix products  7 us (2%)
  local copies, waits for them, and re-layouts  6.1 us (1%)
    reduce_scatter x1, waiting for transfers between devices, body(): lax.psum_scatter(lax.dot_general(out_weight, attended, (((1,), (1,)), (()...  144 us
    all_gather x1, blocking collectives, entering(): lax.all_gather(part.astype(kind), axis)  117 us
    select_n x64, other arithmetic, turn(): return jax.tree.map(lambda a, b: jnp.where(reached, a, b), new, before)  66.6 us
    mul x64, other arithmetic, compose(): later_map[0] * earlier_map[1] + later_map[1]  43.9 us
  transfers between devices with their start and end apart: 3, of which 2 were waited for; matrix products, arithmetic and copies ran while one was open for 1% of the time, Pallas kernels for 0%

commit v1 on v0

v1 whole, which is shorter than its diff:
```python
import functools

import jax
import jax.numpy as jnp
from jax import lax
from jax.experimental import pallas as pl
from jax.experimental.pallas import tpu as pltpu
from jax.sharding import PartitionSpec as P

HEAD = 128
MESH = pl.DeviceIdType.MESH
XS, YS, ZLO, ZS = 4, 4, 8, 16
GROUP = 8
TOK = 512
COLS = 256
STATE = 256
SLICE = STATE // GROUP
ROWS = 256
TILE = 256
CHUNK = 128
NCHUNK = TOK // CHUNK
EXP2_SCALE = HEAD**-0.5 * 1.4426950408889634
F32 = jnp.float32
BF16 = jnp.bfloat16


def device(x, y, z, c):
    return ((z // ZLO) * XS + x, (z % ZLO) * GROUP + y * 2 + c)


def nt(a, b):
    return lax.dot_general(a, b, (((1,), (1,)), ((), ())), preferred_element_type=F32)


def nn(a, b):
    return lax.dot_general(a, b, (((1,), (0,)), ((), ())), preferred_element_type=F32)


def remote(src, dst, send, recv, target):
    return pltpu.make_async_remote_copy(
        src_ref=src, dst_ref=dst, send_sem=send, recv_sem=recv, device_id=target, device_id_type=MESH
    )


def kernel(
    q_hbm, k_hbm, v_hbm, sq_hbm, g_hbm, w_hbm, o_ref,
    q, k, v, sq, vt, kprev, vprev, gates, asend, arecv, tsend, trecv, ktsend, ktrecv,
    enter, gain, csend, mem, wbuf, top, total, acc, xatt, zsend, zrecv, own,
    lsem, wl_sem, as_sem, ar_sem, gs_sem, gr_sem, kvs_sem, kvr_sem, ws_sem, wr_sem,
    bs_sem, br_sem, bks_sem, bkr_sem, cs_sem, cr_sem, xs_sem, xr_sem, zs_sem, zr_sem, ready,
):
    dp = lax.axis_index("dp")
    seq = lax.axis_index("seq")
    x = dp % XS
    zlo = seq // GROUP
    z = (dp // XS) * ZLO + zlo
    r = seq % GROUP
    y = r // 2
    c = r % 2
    partner = ((dp + XS) % (2 * XS), seq)

    def in_group(j):
        other = (r + j) % GROUP
        return other, (dp, zlo * GROUP + other)

    def on_x(j):
        other = (x + j) % XS
        return other, ((dp // XS) * XS + other, seq)

    last_of_plane = (r == GROUP - 1) & (zlo < ZLO - 1)
    first_of_plane = (r == 0) & (zlo > 0)

    barrier = pltpu.get_barrier_semaphore()
    greeted = [in_group(j)[1] for j in range(1, GROUP)]
    greeted += [on_x(j)[1] for j in range(1, XS)]
    greeted += [device(x, y, (z + d) % ZS, c) for d in (1, 2, 3, 4, 12, 13, 14, 15)]
    for target in greeted:
        pl.semaphore_signal(barrier, inc=1, device_id=target, device_id_type=MESH)

    @pl.when(last_of_plane)
    def _():
        pl.semaphore_signal(barrier, inc=1, device_id=(dp, seq + 1), device_id_type=MESH)

    @pl.when(first_of_plane)
    def _():
        pl.semaphore_signal(barrier, inc=1, device_id=(dp, seq - 1), device_id_type=MESH)

    loads = [
        pltpu.make_async_copy(src, dst, lsem.at[i])
        for i, (src, dst) in enumerate(
            ((k_hbm, k), (sq_hbm, sq), (v_hbm, v), (g_hbm, gates.at[r]), (q_hbm, q))
        )
    ]
    for copy in loads:
        copy.start()
    own_rows = pl.ds(pl.multiple_of(dp * ROWS, ROWS), ROWS)
    partner_rows = pl.ds(pl.multiple_of(partner[0] * ROWS, ROWS), ROWS)
    own_cols = pl.ds(pl.multiple_of(x * COLS, COLS), COLS)
    w_loads = [
        pltpu.make_async_copy(w_hbm.at[own_rows], wbuf.at[0, :, own_cols], wl_sem.at[0]),
        pltpu.make_async_copy(w_hbm.at[partner_rows], wbuf.at[1, :, own_cols], wl_sem.at[1]),
    ]
    for copy in w_loads:
        copy.start()

    loads[0].wait()
    loads[1].wait()
    loads[2].wait()
    loads[3].wait()
    vt[...] = v[...].T
    keep_own = jax.nn.sigmoid(gates[r])
    for h in range(2):
        cols = slice(h * HEAD, (h + 1) * HEAD)
        scores = nt(k[:, cols], sq[:, cols])
        highest = jnp.max(scores, axis=0, keepdims=True)
        weights = jnp.exp2(scores * EXP2_SCALE - highest * EXP2_SCALE)
        sums = jnp.sum(weights, axis=0, keepdims=True)
        update = nn(vt[cols, :], weights.astype(BF16)) / sums
        asend[:, cols] = ((1.0 - keep_own[:, cols]) * update.T).astype(BF16)

    pl.semaphore_wait(
        barrier,
        len(greeted) + last_of_plane.astype(jnp.int32) + first_of_plane.astype(jnp.int32),
    )
    pl.semaphore_signal(
        ready, inc=1, device_id=device(x, y, (z + ZS - 4) % ZS, c), device_id_type=MESH
    )

    slice_rows = pl.ds(pl.multiple_of(r * SLICE, SLICE), SLICE)
    a_copies, g_copies, w_copies = [], [], []
    for j in range(1, GROUP):
        other, target = in_group(j)
        rows = pl.ds(pl.multiple_of(other * SLICE, SLICE), SLICE)
        a_copies.append(
            remote(asend.at[rows], arecv.at[r], as_sem.at[j], ar_sem.at[j], target)
        )
        g_copies.append(remote(g_hbm, gates.at[r], gs_sem.at[j], gr_sem.at[j], target))
        g_copies[-1].start()
        a_copies[-1].start()
    for j in (1, 3, 2):
        other, target = on_x(j)
        base = (dp // XS) * XS
        for part, owner in ((0, base + other), (1, (base + XS) % (2 * XS) + other)):
            rows = pl.ds(pl.multiple_of(owner * ROWS, ROWS), ROWS)
            w_copies.append(
                remote(
                    w_hbm.at[rows], wbuf.at[part, :, own_cols],
                    ws_sem.at[j, part], wr_sem.at[j, part], target,
                )
            )
            w_copies[-1].start()

    kv_copies = [
        remote(src, dst, kvs_sem.at[i], kvr_sem.at[i], (dp, jnp.minimum(seq + 1, 63)))
        for i, (src, dst) in enumerate(((k_hbm, kprev), (v_hbm, vprev)))
    ]

    @pl.when(seq < 63)
    def _():
        for copy in kv_copies:
            copy.start()

    arecv[r] = asend[slice_rows, :]

    loads[4].wait()

    def token_part(keys, values_t, h, t, low, high, later, first):
        cols = slice(h * HEAD, (h + 1) * HEAD)
        toks = slice(t * TILE, (t + 1) * TILE)
        scores = nt(keys[low:high, cols], q[toks, cols])
        key_at = lax.broadcasted_iota(jnp.int32, scores.shape, 0) + low
        tok_at = lax.broadcasted_iota(jnp.int32, scores.shape, 1) + t * TILE
        seen = key_at > tok_at if later else key_at <= tok_at
        scores = jnp.where(seen, scores * EXP2_SCALE, -1e30)
        highest = jnp.max(scores, axis=0, keepdims=True)
        if not first:
            before = top[h, :, toks]
            highest = jnp.maximum(highest, before)
            fade = jnp.exp2(before - highest)
        weights = jnp.exp2(scores - highest)
        sums = jnp.sum(weights, axis=0, keepdims=True)
        summed = nn(values_t[cols, low:high], weights.astype(BF16))
        top[h, :, toks] = highest
        if first:
            total[h, :, toks] = sums
            acc[cols, toks] = summed
        else:
            total[h, :, toks] = fade * total[h, :, toks] + sums
            acc[cols, toks] = fade * acc[cols, toks] + summed

    for h in range(2):
        for t in range(TOK // TILE):
            token_part(k, vt, h, t, 0, (t + 1) * TILE, False, True)

    for copy in g_copies:
        copy.wait_recv()
    for copy in a_copies:
        copy.wait_recv()
    run_v = jnp.zeros((SLICE, COLS), F32)
    run_k = jnp.ones((1, COLS), F32)
    inner = []
    for b in range(GROUP):
        inner.append((run_k, run_v))
        keep = jax.nn.sigmoid(gates[b])
        run_v = keep * run_v + arecv[b].astype(F32)
        run_k = keep * run_k
    tsend[...] = run_v.astype(BF16)
    ktsend[...] = run_k

    def to_plane(d):
        target = (dp, jnp.minimum(zlo + d, ZLO - 1) * GROUP + r)
        return (
            remote(tsend, trecv.at[d - 1], bs_sem.at[d - 1], br_sem.at[d - 1], target),
            remote(ktsend, ktrecv.at[d - 1], bks_sem.at[d - 1], bkr_sem.at[d - 1], target),
        )

    b_copies = [to_plane(d) for d in range(1, ZLO)]
    for d in range(1, ZLO):
        if d == 5:
            pl.semaphore_wait(ready, 1)

        @pl.when(zlo + d < ZLO)
        def _():
            for copy in b_copies[d - 1]:
                copy.start()

    enter[...] = jnp.zeros_like(enter)
    gain[...] = jnp.ones_like(gain)
    for d in range(1, ZLO):

        @pl.when(zlo >= d)
        def _():
            for copy in b_copies[d - 1]:
                copy.wait_recv()
            enter[...] += gain[...] * trecv[d - 1].astype(F32)
            gain[...] = gain[...] * ktrecv[d - 1]

    for b in range(GROUP):
        inner_k, inner_v = inner[b]
        csend[b] = (inner_k * enter[...] + inner_v).astype(BF16)
    c_copies = []
    for j in range(1, GROUP):
        other, target = in_group(j)
        c_copies.append(
            remote(csend.at[other], mem.at[slice_rows], cs_sem.at[j], cr_sem.at[j], target)
        )
        c_copies[-1].start()
    mem[slice_rows, :] = csend[r]

    @pl.when(seq > 0)
    def _():
        for copy in kv_copies:
            copy.wait_recv()
        vt[...] = vprev[...].T
        for h in range(2):
            for t in range(TOK // TILE):
                token_part(kprev, vt, h, t, t * TILE, TOK, True, False)

    for copy in c_copies:
        copy.wait_recv()
    mem_t = mem[...].T
    x_rows = pl.ds(pl.multiple_of(x * COLS, COLS), COLS)
    x_copies = []
    for n in range(NCHUNK):
        toks = slice(n * CHUNK, (n + 1) * CHUNK)
        for h in range(2):
            cols = slice(h * HEAD, (h + 1) * HEAD)
            scores = nt(mem[:, cols], q[toks, cols]) * EXP2_SCALE
            before = top[h, :, toks]
            highest = jnp.maximum(jnp.max(scores, axis=0, keepdims=True), before)
            fade = jnp.exp2(before - highest)
            weights = jnp.exp2(scores - highest)
            sums = fade * total[h, :, toks] + jnp.sum(weights, axis=0, keepdims=True)
            summed = fade * acc[cols, toks] + nn(mem_t[cols, :], weights.astype(BF16))
            xatt[n, pl.ds(pl.multiple_of(x * COLS + h * HEAD, HEAD), HEAD), :] = (
                summed / sums
            ).astype(BF16)
        sent = []
        for j in (1, 3, 2):
            _, target = on_x(j)
            sent.append(
                remote(
                    xatt.at[n, x_rows], xatt.at[n, x_rows], xs_sem.at[n, j], xr_sem.at[n, j], target
                )
            )
            sent[-1].start()
        x_copies.append(sent)

    for copy in w_loads:
        copy.wait()
    for copy in w_copies:
        copy.wait_recv()
    z_copies = []
    for n in range(NCHUNK):
        for copy in x_copies[n]:
            copy.wait_recv()
        zsend[n] = nn(wbuf[1], xatt[n]).astype(BF16)
        z_copies.append(remote(zsend.at[n], zrecv.at[n], zs_sem.at[n], zr_sem.at[n], partner))
        z_copies[-1].start()
    for n in range(NCHUNK):
        own[n] = nn(wbuf[0], xatt[n])
    for n in range(NCHUNK):
        z_copies[n].wait_recv()
        o_ref[:, n * CHUNK : (n + 1) * CHUNK] = (own[n] + zrecv[n].astype(F32)).astype(BF16)

    for copy in g_copies + a_copies + w_copies + c_copies + z_copies:
        copy.wait_send()
    for sent in x_copies:
        for copy in sent:
            copy.wait_send()

    @pl.when(seq < 63)
    def _():
        for copy in kv_copies:
            copy.wait_send()

    for d in range(1, ZLO):

        @pl.when(zlo + d < ZLO)
        def _():
            for copy in b_copies[d - 1]:
                copy.wait_send()


def body(queries, key_rows, value_rows, slot_queries, gate_logit, out_weight):
    dma = pltpu.SemaphoreType.DMA
    vmem = pltpu.VMEM
    return pl.pallas_call(
        kernel,
        out_shape=jax.ShapeDtypeStruct((ROWS, TOK), BF16),
        in_specs=[pl.BlockSpec(memory_space=pl.ANY)] * 6,
        out_specs=pl.BlockSpec(memory_space=pltpu.VMEM),
        scratch_shapes=[
            vmem((TOK, COLS), BF16),
            vmem((TOK, COLS), BF16),
            vmem((TOK, COLS), BF16),
            vmem((STATE, COLS), BF16),
            vmem((COLS, TOK), BF16),
            vmem((TOK, COLS), BF16),
            vmem((TOK, COLS), BF16),
            vmem((GROUP, 1, COLS), F32),
            vmem((STATE, COLS), BF16),
            vmem((GROUP, SLICE, COLS), BF16),
            vmem((SLICE, COLS), BF16),
            vmem((ZLO - 1, SLICE, COLS), BF16),
            vmem((1, COLS), F32),
            vmem((ZLO - 1, 1, COLS), F32),
            vmem((SLICE, COLS), F32),
            vmem((1, COLS), F32),
            vmem((GROUP, SLICE, COLS), BF16),
            vmem((STATE, COLS), BF16),
            vmem((2, ROWS, XS * COLS), BF16),
            vmem((2, 1, TOK), F32),
            vmem((2, 1, TOK), F32),
            vmem((COLS, TOK), F32),
            vmem((NCHUNK, XS * COLS, CHUNK), BF16),
            vmem((NCHUNK, ROWS, CHUNK), BF16),
            vmem((NCHUNK, ROWS, CHUNK), BF16),
            vmem((NCHUNK, ROWS, CHUNK), F32),
            dma((5,)),
            dma((2,)),
            dma((GROUP,)),
            dma((GROUP,)),
            dma((GROUP,)),
            dma((GROUP,)),
            dma((2,)),
            dma((2,)),
            dma((XS, 2)),
            dma((XS, 2)),
            dma((ZLO - 1,)),
            dma((ZLO - 1,)),
            dma((ZLO - 1,)),
            dma((ZLO - 1,)),
            dma((GROUP,)),
            dma((GROUP,)),
            dma((NCHUNK, XS)),
            dma((NCHUNK, XS)),
            dma((NCHUNK,)),
            dma((NCHUNK,)),
            pltpu.SemaphoreType.REGULAR,
        ],
        compiler_params=pltpu.CompilerParams(collective_id=0, has_side_effects=True),
    )(queries, key_rows, value_rows, slot_queries, gate_logit, out_weight)


def solution(mesh):
    in_specs = (
        P("seq", "dp"),
        P("seq", "dp"),
        P("seq", "dp"),
        P(None, "dp"),
        P("seq", "dp"),
        P(None, "dp"),
    )
    return jax.shard_map(
        body, mesh=mesh, in_specs=in_specs, out_specs=P("dp", "seq"), check_vma=False
    )
```

time: 416 us -> 64.2 us (0.15)
  the two profiles are of different devices: /device:TPU:8 before, /device:TPU:161 now
where the time goes in v1:
time: 64.2 us; the launch traced here: 64 us
  Pallas kernels  62.3 us (97%)
  local copies, waits for them, and re-layouts  1.67 us (3%)
    pallas_call x1, Pallas kernels, body(): pl.pallas_call(kernel, out_shape=jax.ShapeDtypeStruct((ROWS, TOK), BF16),...  62.3 us
    unnamed x1, local copies, waits for them, and re-layouts  1.67 us

profile of v1, /device:TPU:161, one launch (start us, length us, event | category | flops | bytes accessed | tf_op | source)
XLA Modules:
  0.0 64.0 jit_solution(14154463201051028895)
XLA Ops:
  0.0 62.3 %shard_map.64 = bf16[256,512]{1,0:T(8,128)(2,1)} custom-call(bf16[512,256]{1,0:T(8,128)(2,1)} %q_hbm.1, bf16[512,256]{1,0:T(8,128)(2,1)} %k_hbm.1, bf16[512,256]{1,0:T(8,128)(2,1)} %v_hbm.1, bf16[256,256]{1,0:T(8,128)(2,1)} %sq_hbm.1, f32[1,256]{1,0:T(1,128)} %g_hbm.1, bf16[2048,256]{1,0:T(8,128)(2,1)} %w_hbm.1), custom_call_target="tpu_custom_call" | custom-call | tf_op jit(solution)/shard_map/pallas_call | solution.py:328
  62.4 1.7 %copy.8 = bf16[256,512]{1,0:T(8,128)(2,1)} copy(bf16[256,512]{1,0:T(8,128)(2,1)} %shard_map.64) | data formatting | bytes 524288

commit v2 on v1

--- a/solution.py
+++ b/solution.py
@@ -15,6 +15,7 @@
 COLS = 256
 STATE = 256
 SLICE = STATE // GROUP
+EXTRA = 16
 ROWS = 256
 TILE = 256
 CHUNK = 128
@@ -36,6 +37,21 @@
     return lax.dot_general(a, b, (((1,), (0,)), ((), ())), preferred_element_type=F32)
 
 
+def in_parts(rate):
+    high = rate.astype(BF16)
+    rest = rate - high.astype(F32)
+    middle = rest.astype(BF16)
+    low = (rest - middle.astype(F32)).astype(BF16)
+    row = lax.broadcasted_iota(jnp.int32, (EXTRA, COLS), 0)
+    wide = [jnp.broadcast_to(part.astype(F32), (EXTRA, COLS)) for part in (high, middle, low)]
+    return jnp.where(row == 0, wide[0], jnp.where(row == 1, wide[1], wide[2])).astype(BF16)
+
+
+def from_parts(rows):
+    wide = rows.astype(F32)
+    return (wide[0:1] + wide[1:2]) + wide[2:3]
+
+
 def remote(src, dst, send, recv, target):
     return pltpu.make_async_remote_copy(
         src_ref=src, dst_ref=dst, send_sem=send, recv_sem=recv, device_id=target, device_id_type=MESH
@@ -44,9 +60,9 @@
 
 def kernel(
     q_hbm, k_hbm, v_hbm, sq_hbm, g_hbm, w_hbm, o_ref,
-    q, k, v, sq, vt, kprev, vprev, gates, asend, arecv, tsend, trecv, ktsend, ktrecv,
+    q, k, v, sq, vt, kprev, vprev, gate, asend, arecv, tsend, trecv, ktsend, ktrecv,
     enter, gain, csend, mem, wbuf, top, total, acc, xatt, zsend, zrecv, own,
-    lsem, wl_sem, as_sem, ar_sem, gs_sem, gr_sem, kvs_sem, kvr_sem, ws_sem, wr_sem,
+    lsem, wl_sem, as_sem, ar_sem, kvs_sem, kvr_sem, ws_sem, wr_sem,
     bs_sem, br_sem, bks_sem, bkr_sem, cs_sem, cr_sem, xs_sem, xr_sem, zs_sem, zr_sem, ready,
 ):
     dp = lax.axis_index("dp")
@@ -70,6 +86,15 @@
     last_of_plane = (r == GROUP - 1) & (zlo < ZLO - 1)
     first_of_plane = (r == 0) & (zlo > 0)
 
+    loads = [
+        pltpu.make_async_copy(src, dst, lsem.at[i])
+        for i, (src, dst) in enumerate(
+            ((k_hbm, k), (sq_hbm, sq), (v_hbm, v), (g_hbm, gate), (q_hbm, q))
+        )
+    ]
+    for copy in loads:
+        copy.start()
+
     barrier = pltpu.get_barrier_semaphore()
     greeted = [in_group(j)[1] for j in range(1, GROUP)]
     greeted += [on_x(j)[1] for j in range(1, XS)]
@@ -85,14 +110,6 @@
     def _():
         pl.semaphore_signal(barrier, inc=1, device_id=(dp, seq - 1), device_id_type=MESH)
 
-    loads = [
-        pltpu.make_async_copy(src, dst, lsem.at[i])
-        for i, (src, dst) in enumerate(
-            ((k_hbm, k), (sq_hbm, sq), (v_hbm, v), (g_hbm, gates.at[r]), (q_hbm, q))
-        )
-    ]
-    for copy in loads:
-        copy.start()
     own_rows = pl.ds(pl.multiple_of(dp * ROWS, ROWS), ROWS)
     partner_rows = pl.ds(pl.multiple_of(partner[0] * ROWS, ROWS), ROWS)
     own_cols = pl.ds(pl.multiple_of(x * COLS, COLS), COLS)
@@ -108,7 +125,8 @@
     loads[2].wait()
     loads[3].wait()
     vt[...] = v[...].T
-    keep_own = jax.nn.sigmoid(gates[r])
+    keep_own = jax.nn.sigmoid(gate[...])
+    parts = in_parts(keep_own)
     for h in range(2):
         cols = slice(h * HEAD, (h + 1) * HEAD)
         scores = nt(k[:, cols], sq[:, cols])
@@ -116,7 +134,11 @@
         weights = jnp.exp2(scores * EXP2_SCALE - highest * EXP2_SCALE)
         sums = jnp.sum(weights, axis=0, keepdims=True)
         update = nn(vt[cols, :], weights.astype(BF16)) / sums
-        asend[:, cols] = ((1.0 - keep_own[:, cols]) * update.T).astype(BF16)
+        kept = ((1.0 - keep_own[:, cols]) * update.T).astype(BF16)
+        for b in range(GROUP):
+            asend[b, :SLICE, cols] = kept[b * SLICE : (b + 1) * SLICE]
+    for b in range(GROUP):
+        asend[b, SLICE:, :] = parts
 
     pl.semaphore_wait(
         barrier,
@@ -127,15 +149,12 @@
     )
 
     slice_rows = pl.ds(pl.multiple_of(r * SLICE, SLICE), SLICE)
-    a_copies, g_copies, w_copies = [], [], []
+    a_copies, w_copies = [], []
     for j in range(1, GROUP):
         other, target = in_group(j)
-        rows = pl.ds(pl.multiple_of(other * SLICE, SLICE), SLICE)
         a_copies.append(
-            remote(asend.at[rows], arecv.at[r], as_sem.at[j], ar_sem.at[j], target)
+            remote(asend.at[other], arecv.at[r], as_sem.at[j], ar_sem.at[j], target)
         )
-        g_copies.append(remote(g_hbm, gates.at[r], gs_sem.at[j], gr_sem.at[j], target))
-        g_copies[-1].start()
         a_copies[-1].start()
     for j in (1, 3, 2):
         other, target = on_x(j)
@@ -160,7 +179,7 @@
         for copy in kv_copies:
             copy.start()
 
-    arecv[r] = asend[slice_rows, :]
+    arecv[r] = asend[r]
 
     loads[4].wait()
 
@@ -192,8 +211,6 @@
         for t in range(TOK // TILE):
             token_part(k, vt, h, t, 0, (t + 1) * TILE, False, True)
 
-    for copy in g_copies:
-        copy.wait_recv()
     for copy in a_copies:
         copy.wait_recv()
     run_v = jnp.zeros((SLICE, COLS), F32)
@@ -201,8 +218,8 @@
     inner = []
     for b in range(GROUP):
         inner.append((run_k, run_v))
-        keep = jax.nn.sigmoid(gates[b])
-        run_v = keep * run_v + arecv[b].astype(F32)
+        keep = from_parts(arecv[b, SLICE:, :])
+        run_v = keep * run_v + arecv[b, :SLICE, :].astype(F32)
         run_k = keep * run_k
     tsend[...] = run_v.astype(BF16)
     ktsend[...] = run_k
@@ -303,7 +320,7 @@
         z_copies[n].wait_recv()
         o_ref[:, n * CHUNK : (n + 1) * CHUNK] = (own[n] + zrecv[n].astype(F32)).astype(BF16)
 
-    for copy in g_copies + a_copies + w_copies + c_copies + z_copies:
+    for copy in a_copies + w_copies + c_copies + z_copies:
         copy.wait_send()
     for sent in x_copies:
         for copy in sent:
@@ -327,7 +344,7 @@
     vmem = pltpu.VMEM
     return pl.pallas_call(
         kernel,
-        out_shape=jax.ShapeDtypeStruct((ROWS, TOK), BF16),
+        out_shape=pltpu.VMEM((ROWS, TOK), BF16),
         in_specs=[pl.BlockSpec(memory_space=pl.ANY)] * 6,
         out_specs=pl.BlockSpec(memory_space=pltpu.VMEM),
         scratch_shapes=[
@@ -338,9 +355,9 @@
             vmem((COLS, TOK), BF16),
             vmem((TOK, COLS), BF16),
             vmem((TOK, COLS), BF16),
-            vmem((GROUP, 1, COLS), F32),
-            vmem((STATE, COLS), BF16),
-            vmem((GROUP, SLICE, COLS), BF16),
+            vmem((1, COLS), F32),
+            vmem((GROUP, SLICE + EXTRA, COLS), BF16),
+            vmem((GROUP, SLICE + EXTRA, COLS), BF16),
             vmem((SLICE, COLS), BF16),
             vmem((ZLO - 1, SLICE, COLS), BF16),
             vmem((1, COLS), F32),
@@ -361,8 +378,6 @@
             dma((2,)),
             dma((GROUP,)),
             dma((GROUP,)),
-            dma((GROUP,)),
-            dma((GROUP,)),
             dma((2,)),
             dma((2,)),
             dma((XS, 2)),

time: 64.2 us -> 62.6 us (0.975)
  the two profiles are of different devices: /device:TPU:161 before, /device:TPU:160 now
where the time goes in v2:
time: 62.6 us; the launch traced here: 62.4 us
  Pallas kernels  61.7 us (99%)
  local copies, waits for them, and re-layouts  0.71 us (1%)
    pallas_call x1, Pallas kernels, body(): pl.pallas_call(kernel, out_shape=pltpu.VMEM((ROWS, TOK), BF16), in_specs=...  61.7 us

profile of v2, /device:TPU:160, one launch (start us, length us, event | category | flops | bytes accessed | tf_op | source)
XLA Modules:
  0.0 62.4 jit_solution(8890204019656243247)
XLA Ops:
  0.0 61.7 %shard_map.64 = bf16[256,512]{1,0:T(8,128)(2,1)S(1)} custom-call(bf16[512,256]{1,0:T(8,128)(2,1)} %q_hbm.1, bf16[512,256]{1,0:T(8,128)(2,1)} %k_hbm.1, bf16[512,256]{1,0:T(8,128)(2,1)} %v_hbm.1, bf16[256,256]{1,0:T(8,128)(2,1)} %sq_hbm.1, f32[1,256]{1,0:T(1,128)} %g_hbm.1, bf16[2048,256]{1,0:T(8,128)(2,1)} %w_hbm.1), custom_call_target="tpu_custom_call" | custom-call | tf_op jit(solution)/shard_map/pallas_call | solution.py:345
  61.7 0.7 %copy.8 = bf16[256,512]{1,0:T(8,128)(2,1)} copy(bf16[256,512]{1,0:T(8,128)(2,1)S(1)} %shard_map.64) | data formatting | bytes 524288

commit v3 on v2

--- a/solution.py
+++ b/solution.py
@@ -98,7 +98,7 @@
     barrier = pltpu.get_barrier_semaphore()
     greeted = [in_group(j)[1] for j in range(1, GROUP)]
     greeted += [on_x(j)[1] for j in range(1, XS)]
-    greeted += [device(x, y, (z + d) % ZS, c) for d in (1, 2, 3, 4, 12, 13, 14, 15)]
+    greeted += [device(x, y, (z + d) % ZS, c) for d in (1, 15)]
     for target in greeted:
         pl.semaphore_signal(barrier, inc=1, device_id=target, device_id_type=MESH)
 
@@ -144,10 +144,14 @@
         barrier,
         len(greeted) + last_of_plane.astype(jnp.int32) + first_of_plane.astype(jnp.int32),
     )
-    pl.semaphore_signal(
-        ready, inc=1, device_id=device(x, y, (z + ZS - 4) % ZS, c), device_id_type=MESH
-    )
-
+
+    def tell(n):
+        for d in (1 << n, ZS - (1 << n)):
+            pl.semaphore_signal(
+                ready.at[n], inc=1, device_id=device(x, y, (z + d) % ZS, c), device_id_type=MESH
+            )
+
+    tell(0)
     slice_rows = pl.ds(pl.multiple_of(r * SLICE, SLICE), SLICE)
     a_copies, w_copies = [], []
     for j in range(1, GROUP):
@@ -180,6 +184,9 @@
             copy.start()
 
     arecv[r] = asend[r]
+
+    pl.semaphore_wait(ready.at[0], 2)
+    tell(1)
 
     loads[4].wait()
 
@@ -211,6 +218,9 @@
         for t in range(TOK // TILE):
             token_part(k, vt, h, t, 0, (t + 1) * TILE, False, True)
 
+    pl.semaphore_wait(ready.at[1], 2)
+    tell(2)
+
     for copy in a_copies:
         copy.wait_recv()
     run_v = jnp.zeros((SLICE, COLS), F32)
@@ -234,7 +244,7 @@
     b_copies = [to_plane(d) for d in range(1, ZLO)]
     for d in range(1, ZLO):
         if d == 5:
-            pl.semaphore_wait(ready, 1)
+            pl.semaphore_wait(ready.at[2], 2)
 
         @pl.when(zlo + d < ZLO)
         def _():
@@ -392,7 +402,7 @@
             dma((NCHUNK, XS)),
             dma((NCHUNK,)),
             dma((NCHUNK,)),
-            pltpu.SemaphoreType.REGULAR,
+            pltpu.SemaphoreType.REGULAR((3,)),
         ],
         compiler_params=pltpu.CompilerParams(collective_id=0, has_side_effects=True),
     )(queries, key_rows, value_rows, slot_queries, gate_logit, out_weight)

time: 62.6 us -> 61 us (0.974)
  the two profiles are of different devices: /device:TPU:160 before, /device:TPU:193 now
where the time goes in v3:
time: 61 us; the launch traced here: 60.9 us
  Pallas kernels  60.2 us (99%)
  local copies, waits for them, and re-layouts  0.71 us (1%)
    pallas_call x1, Pallas kernels, body(): pl.pallas_call(kernel, out_shape=pltpu.VMEM((ROWS, TOK), BF16), in_specs=...  60.2 us

profile of v3, /device:TPU:193, one launch (start us, length us, event | category | flops | bytes accessed | tf_op | source)
XLA Modules:
  0.0 60.9 jit_solution(3182807784967387621)
XLA Ops:
  0.0 60.2 %shard_map.64 = bf16[256,512]{1,0:T(8,128)(2,1)S(1)} custom-call(bf16[512,256]{1,0:T(8,128)(2,1)} %q_hbm.1, bf16[512,256]{1,0:T(8,128)(2,1)} %k_hbm.1, bf16[512,256]{1,0:T(8,128)(2,1)} %v_hbm.1, bf16[256,256]{1,0:T(8,128)(2,1)} %sq_hbm.1, f32[1,256]{1,0:T(1,128)} %g_hbm.1, bf16[2048,256]{1,0:T(8,128)(2,1)} %w_hbm.1), custom_call_target="tpu_custom_call" | custom-call | tf_op jit(solution)/shard_map/pallas_call | solution.py:355
  60.2 0.7 %copy.8 = bf16[256,512]{1,0:T(8,128)(2,1)} copy(bf16[256,512]{1,0:T(8,128)(2,1)S(1)} %shard_map.64) | data formatting | bytes 524288

commit v4 on v3

--- a/solution.py
+++ b/solution.py
@@ -154,7 +154,7 @@
     tell(0)
     slice_rows = pl.ds(pl.multiple_of(r * SLICE, SLICE), SLICE)
     a_copies, w_copies = [], []
-    for j in range(1, GROUP):
+    for j in (2, 6, 4, 1, 3, 5, 7):
         other, target = in_group(j)
         a_copies.append(
             remote(asend.at[other], arecv.at[r], as_sem.at[j], ar_sem.at[j], target)
@@ -266,7 +266,7 @@
         inner_k, inner_v = inner[b]
         csend[b] = (inner_k * enter[...] + inner_v).astype(BF16)
     c_copies = []
-    for j in range(1, GROUP):
+    for j in (2, 6, 4, 1, 7, 3, 5):
         other, target = in_group(j)
         c_copies.append(
             remote(csend.at[other], mem.at[slice_rows], cs_sem.at[j], cr_sem.at[j], target)

time: 61 us -> 60.3 us (0.989)
  Pallas kernels: 60.2 us -> 59.5 us
    pallas_call x1, Pallas kernels: 60.2 us -> 59.5 us  [body(): pl.pallas_call(kernel, out_shape=pltpu.VMEM((ROWS, TOK), BF16), in_specs=...]
where the time goes in v4:
time: 60.3 us; the launch traced here: 60.2 us
  Pallas kernels  59.5 us (99%)
  local copies, waits for them, and re-layouts  0.71 us (1%)
    pallas_call x1, Pallas kernels, body(): pl.pallas_call(kernel, out_shape=pltpu.VMEM((ROWS, TOK), BF16), in_specs=...  59.5 us

profile of v4, /device:TPU:193, one launch (start us, length us, event | category | flops | bytes accessed | tf_op | source)
XLA Modules:
  0.0 60.2 jit_solution(5960558167403005356)
XLA Ops:
  0.0 59.5 %shard_map.64 = bf16[256,512]{1,0:T(8,128)(2,1)S(1)} custom-call(bf16[512,256]{1,0:T(8,128)(2,1)} %q_hbm.1, bf16[512,256]{1,0:T(8,128)(2,1)} %k_hbm.1, bf16[512,256]{1,0:T(8,128)(2,1)} %v_hbm.1, bf16[256,256]{1,0:T(8,128)(2,1)} %sq_hbm.1, f32[1,256]{1,0:T(1,128)} %g_hbm.1, bf16[2048,256]{1,0:T(8,128)(2,1)} %w_hbm.1), custom_call_target="tpu_custom_call" | custom-call | tf_op jit(solution)/shard_map/pallas_call | solution.py:355
  59.5 0.7 %copy.8 = bf16[256,512]{1,0:T(8,128)(2,1)} copy(bf16[256,512]{1,0:T(8,128)(2,1)S(1)} %shard_map.64) | data formatting | bytes 524288

commit v5 on v4

--- a/solution.py
+++ b/solution.py
@@ -11,6 +11,7 @@
 MESH = pl.DeviceIdType.MESH
 XS, YS, ZLO, ZS = 4, 4, 8, 16
 GROUP = 8
+QUAD = 4
 TOK = 512
 COLS = 256
 STATE = 256
@@ -60,10 +61,10 @@
 
 def kernel(
     q_hbm, k_hbm, v_hbm, sq_hbm, g_hbm, w_hbm, o_ref,
-    q, k, v, sq, vt, kprev, vprev, gate, asend, arecv, tsend, trecv, ktsend, ktrecv,
+    q, k, v, sq, vt, kprev, vprev, gate, asend, arecv, tsend, trecv, ktsend, ktrecv, usend, urecv,
     enter, gain, csend, mem, wbuf, top, total, acc, xatt, zsend, zrecv, own,
     lsem, wl_sem, as_sem, ar_sem, kvs_sem, kvr_sem, ws_sem, wr_sem,
-    bs_sem, br_sem, bks_sem, bkr_sem, cs_sem, cr_sem, xs_sem, xr_sem, zs_sem, zr_sem, ready,
+    bs_sem, br_sem, bks_sem, bkr_sem, us_sem, ur_sem, cs_sem, cr_sem, xs_sem, xr_sem, zs_sem, zr_sem, ready,
 ):
     dp = lax.axis_index("dp")
     seq = lax.axis_index("seq")
@@ -241,26 +242,45 @@
             remote(ktsend, ktrecv.at[d - 1], bks_sem.at[d - 1], bkr_sem.at[d - 1], target),
         )
 
-    b_copies = [to_plane(d) for d in range(1, ZLO)]
-    for d in range(1, ZLO):
-        if d == 5:
-            pl.semaphore_wait(ready.at[2], 2)
-
-        @pl.when(zlo + d < ZLO)
+    b_copies = [to_plane(d) for d in range(1, QUAD)]
+    u_copies = [
+        remote(
+            usend, urecv, us_sem.at[d - 1], ur_sem.at[d - 1],
+            (dp, jnp.minimum(zlo + d, ZLO - 1) * GROUP + r),
+        )
+        for d in range(1, QUAD + 1)
+    ]
+    place = zlo % QUAD
+    for d in range(1, QUAD):
+
+        @pl.when(place + d < QUAD)
         def _():
             for copy in b_copies[d - 1]:
                 copy.start()
 
     enter[...] = jnp.zeros_like(enter)
     gain[...] = jnp.ones_like(gain)
-    for d in range(1, ZLO):
-
-        @pl.when(zlo >= d)
+    for d in range(1, QUAD):
+
+        @pl.when(place >= d)
         def _():
             for copy in b_copies[d - 1]:
                 copy.wait_recv()
             enter[...] += gain[...] * trecv[d - 1].astype(F32)
             gain[...] = gain[...] * ktrecv[d - 1]
+
+    @pl.when(zlo == QUAD - 1)
+    def _():
+        usend[...] = (run_k * enter[...] + run_v).astype(BF16)
+        for copy in u_copies:
+            copy.start()
+
+    for d in range(1, QUAD + 1):
+
+        @pl.when(zlo == QUAD - 1 + d)
+        def _():
+            u_copies[d - 1].wait_recv()
+            enter[...] += gain[...] * urecv[...].astype(F32)
 
     for b in range(GROUP):
         inner_k, inner_v = inner[b]
@@ -273,6 +293,7 @@
         )
         c_copies[-1].start()
     mem[slice_rows, :] = csend[r]
+    pl.semaphore_wait(ready.at[2], 2)
 
     @pl.when(seq > 0)
     def _():
@@ -341,12 +362,17 @@
         for copy in kv_copies:
             copy.wait_send()
 
-    for d in range(1, ZLO):
-
-        @pl.when(zlo + d < ZLO)
+    for d in range(1, QUAD):
+
+        @pl.when(place + d < QUAD)
         def _():
             for copy in b_copies[d - 1]:
                 copy.wait_send()
+
+    @pl.when(zlo == QUAD - 1)
+    def _():
+        for copy in u_copies:
+            copy.wait_send()
 
 
 def body(queries, key_rows, value_rows, slot_queries, gate_logit, out_weight):
@@ -369,9 +395,11 @@
             vmem((GROUP, SLICE + EXTRA, COLS), BF16),
             vmem((GROUP, SLICE + EXTRA, COLS), BF16),
             vmem((SLICE, COLS), BF16),
-            vmem((ZLO - 1, SLICE, COLS), BF16),
+            vmem((QUAD - 1, SLICE, COLS), BF16),
             vmem((1, COLS), F32),
-            vmem((ZLO - 1, 1, COLS), F32),
+            vmem((QUAD - 1, 1, COLS), F32),
+            vmem((SLICE, COLS), BF16),
+            vmem((SLICE, COLS), BF16),
             vmem((SLICE, COLS), F32),
             vmem((1, COLS), F32),
             vmem((GROUP, SLICE, COLS), BF16),
@@ -392,10 +420,12 @@
             dma((2,)),
             dma((XS, 2)),
             dma((XS, 2)),
-            dma((ZLO - 1,)),
-            dma((ZLO - 1,)),
-            dma((ZLO - 1,)),
-            dma((ZLO - 1,)),
+            dma((QUAD - 1,)),
+            dma((QUAD - 1,)),
+            dma((QUAD - 1,)),
+            dma((QUAD - 1,)),
+            dma((QUAD,)),
+            dma((QUAD,)),
             dma((GROUP,)),
             dma((GROUP,)),
             dma((NCHUNK, XS)),

time: 60.3 us -> 59.7 us (0.990)
  Pallas kernels: 59.5 us -> 58.8 us
    pallas_call x1, Pallas kernels: 59.5 us -> 58.8 us  [body(): pl.pallas_call(kernel, out_shape=pltpu.VMEM((ROWS, TOK), BF16), in_specs=...]
where the time goes in v5:
time: 59.7 us; the launch traced here: 59.6 us
  Pallas kernels  58.8 us (98%)
  local copies, waits for them, and re-layouts  0.71 us (1%)
    pallas_call x1, Pallas kernels, body(): pl.pallas_call(kernel, out_shape=pltpu.VMEM((ROWS, TOK), BF16), in_specs=...  58.8 us

profile of v5, /device:TPU:193, one launch (start us, length us, event | category | flops | bytes accessed | tf_op | source)
XLA Modules:
  0.0 59.6 jit_solution(5550092172199203365)
XLA Ops:
  0.0 58.8 %shard_map.64 = bf16[256,512]{1,0:T(8,128)(2,1)S(1)} custom-call(bf16[512,256]{1,0:T(8,128)(2,1)} %q_hbm.1, bf16[512,256]{1,0:T(8,128)(2,1)} %k_hbm.1, bf16[512,256]{1,0:T(8,128)(2,1)} %v_hbm.1, bf16[256,256]{1,0:T(8,128)(2,1)} %sq_hbm.1, f32[1,256]{1,0:T(1,128)} %g_hbm.1, bf16[2048,256]{1,0:T(8,128)(2,1)} %w_hbm.1), custom_call_target="tpu_custom_call" | custom-call | tf_op jit(solution)/shard_map/pallas_call | solution.py:381
  58.9 0.7 %copy.8 = bf16[256,512]{1,0:T(8,128)(2,1)} copy(bf16[256,512]{1,0:T(8,128)(2,1)S(1)} %shard_map.64) | data formatting | bytes 524288

commit v6 on v5

--- a/solution.py
+++ b/solution.py
@@ -293,7 +293,6 @@
         )
         c_copies[-1].start()
     mem[slice_rows, :] = csend[r]
-    pl.semaphore_wait(ready.at[2], 2)
 
     @pl.when(seq > 0)
     def _():
@@ -334,6 +333,7 @@
             sent[-1].start()
         x_copies.append(sent)
 
+    pl.semaphore_wait(ready.at[2], 2)
     for copy in w_loads:
         copy.wait()
     for copy in w_copies:

time: 59.7 us -> 59.7 us (level)
  the two profiles are of different devices: /device:TPU:193 before, /device:TPU:209 now
where the time goes in v6:
time: 59.7 us; the launch traced here: 59.6 us
  Pallas kernels  58.9 us (99%)
  local copies, waits for them, and re-layouts  0.71 us (1%)
    pallas_call x1, Pallas kernels, body(): pl.pallas_call(kernel, out_shape=pltpu.VMEM((ROWS, TOK), BF16), in_specs=...  58.9 us

profile of v6, /device:TPU:209, one launch (start us, length us, event | category | flops | bytes accessed | tf_op | source)
XLA Modules:
  0.0 59.6 jit_solution(9374255765045492083)
XLA Ops:
  0.0 58.9 %shard_map.64 = bf16[256,512]{1,0:T(8,128)(2,1)S(1)} custom-call(bf16[512,256]{1,0:T(8,128)(2,1)} %q_hbm.1, bf16[512,256]{1,0:T(8,128)(2,1)} %k_hbm.1, bf16[512,256]{1,0:T(8,128)(2,1)} %v_hbm.1, bf16[256,256]{1,0:T(8,128)(2,1)} %sq_hbm.1, f32[1,256]{1,0:T(1,128)} %g_hbm.1, bf16[2048,256]{1,0:T(8,128)(2,1)} %w_hbm.1), custom_call_target="tpu_custom_call" | custom-call | tf_op jit(solution)/shard_map/pallas_call | solution.py:381
  58.9 0.7 %copy.8 = bf16[256,512]{1,0:T(8,128)(2,1)} copy(bf16[256,512]{1,0:T(8,128)(2,1)S(1)} %shard_map.64) | data formatting | bytes 524288
